TPU v7x, 256 devices: a whole 4x4x8 slice. The times are simulated.
256 devices in a mesh: leaf: 64 (over z, x, core), level: 4 (over y).
Axes of the slice: x: 4, y: 4, z: 8, core: 2. Of those that a mesh axis runs over, the one named last changes fastest.
Arguments:
- charges: bfloat16 [3072, 128, 256], P(('leaf', 'level')), may hold values from -6 to 6
- near_mat: bfloat16 [3072, 16, 128, 128], P(('leaf', 'level')), may hold values from -0.1875 to 0.1875
- near_source: int32 [3072, 16], P(('leaf', 'level')), may hold values from 0 to 143
- near_count: int32 [3072], P(('leaf', 'level')), may hold values from 1 to 16, as said below
- moment_map: bfloat16 [3072, 256, 128], P(('leaf', 'level')), may hold values from -0.078125 to 0.078125
- local_eval: bfloat16 [3072, 128, 256], P(('leaf', 'level')), may hold values from -0.375 to 0.375
- upward_child_translation: bfloat16 [8, 256, 256], replicated, may hold values from -0.125 to 0.125
- shift_down: bfloat16 [8, 256, 256], replicated, may hold values from -0.375 to 0.375
- transfer_ops: bfloat16 [8, 256, 256], replicated, may hold values from -0.0625 to 0.0625
- subtree_interaction_list: int32 [64, 32], P('leaf'), may hold values from 0 to 63
- subtree_interaction_operators: int32 [64, 32], P('leaf'), may hold values from 0 to 7
- parent_list: int32 [64, 8], P('leaf'), may hold values from 0 to 7
- parent_ops: int32 [64, 8], P('leaf'), may hold values from 0 to 7
Outputs:
- potential: float32 [3072, 128, 256], P(('leaf', 'level'))
Inputs may be any that keep to these rules, and one draw needn't show every extreme that they name: `near_count`: some block uses all 16 slots and some block only one.
All inputs are finite; a program needn't handle non-finite values.
Results may differ from a plain program's by a relative error of at most 0.012.
Values may be sent and summed in bfloat16 or wider, within the bound.
No kernel may reach another device: no remote copies, remote signals or barrier semaphores. Data moves between devices by JAX's collectives and lax.ppermute only.
A program may use at most 128 MiB of HBM per device.

v0:
```python
import jax
import jax.numpy as jnp
from jax import lax
from jax.sharding import PartitionSpec as P


def extended_2(cells, sides, width):
    for axis, dim in sides:
        count = lax.axis_size(axis)
        ends = count - 1
        head = lax.slice_in_dim(cells, 0, width, axis=dim)
        tail = lax.slice_in_dim(cells, cells.shape[dim] - width, cells.shape[dim], axis=dim)
        cells = jnp.concatenate(
            [
                lax.ppermute(tail, axis, [(i, (i + 1) % count) for i in range(ends)]),
                cells,
                lax.ppermute(head, axis, [((i + 1) % count, i) for i in range(ends)]),
            ],
            axis=dim,
        )
    return cells


def top_tree(
    every,
    upward_child_translation,
    shift_down,
    transfer_ops,
    subtree_interaction_list,
    subtree_interaction_operators,
    parent_list,
    parent_ops,
    leaf_index,
):
    leaves, coeffs, columns = every.shape
    grouped_terms = every.reshape(leaves // 8, 8, coeffs, columns)
    upper_levels = jnp.einsum(
        "get,kgtv->kev", upward_child_translation, grouped_terms, preferred_element_type=jnp.float32
    ).astype(jnp.bfloat16)
    coarse = jnp.einsum(
        "kcd,kdr->cr",
        transfer_ops[parent_ops[0]],
        upper_levels[parent_list[0]],
        preferred_element_type=jnp.float32,
    ).astype(jnp.bfloat16)
    far_leaf = jnp.einsum(
        "kcd,kdr->cr",
        transfer_ops[subtree_interaction_operators[0]],
        every[subtree_interaction_list[0]],
        preferred_element_type=jnp.float32,
    )
    downward = jnp.dot(shift_down[leaf_index % 8], coarse, preferred_element_type=jnp.float32)
    return (far_leaf + downward).astype(jnp.bfloat16)


def on_device(
    charges,
    near_mat,
    near_source,
    near_count,
    moment_map,
    local_eval,
    upward_child_translation,
    shift_down,
    transfer_ops,
    subtree_interaction_list,
    subtree_interaction_operators,
    parent_list,
    parent_ops,
):
    slots = near_mat.shape[1]
    subtree = lax.all_gather(charges, "level", axis=0, tiled=True)
    extended = extended_2(subtree, (("leaf", 0),), subtree.shape[0])
    picked = extended[near_source]
    active = (jnp.arange(slots, dtype=jnp.int32)[None, :] < near_count[:, None]).astype(
        jnp.bfloat16
    )
    picked = picked * active[:, :, None, None]
    near_part = jnp.einsum("bkpq,bkqr->bpr", near_mat, picked, preferred_element_type=jnp.float32)
    partial_moment = jnp.einsum(
        "bcp,bpr->cr", moment_map, charges, preferred_element_type=jnp.float32
    )
    leaf_index = lax.axis_index("leaf")
    moment = lax.psum(partial_moment.astype(jnp.bfloat16), "level")
    every = lax.all_gather(moment[None], "leaf", axis=0, tiled=True)
    local_part = top_tree(
        every,
        upward_child_translation,
        shift_down,
        transfer_ops,
        subtree_interaction_list,
        subtree_interaction_operators,
        parent_list,
        parent_ops,
        leaf_index,
    )
    far_part = jnp.einsum("bpc,cr->bpr", local_eval, local_part, preferred_element_type=jnp.float32)
    return near_part + far_part


def solution(mesh):
    placed = (
        P(("leaf", "level"), None, None),
        P(("leaf", "level"), None, None, None),
        P(("leaf", "level"), None),
        P(("leaf", "level")),
        P(("leaf", "level"), None, None),
        P(("leaf", "level"), None, None),
        P(),
        P(),
        P(),
        P("leaf", None),
        P("leaf", None),
        P("leaf", None),
        P("leaf", None),
    )
    return jax.shard_map(
        on_device,
        mesh=mesh,
        in_specs=placed,
        out_specs=P(("leaf", "level"), None, None),
        check_vma=False,
    )
```

profile of v0, /device:TPU:103, one launch (start us, length us, event | category | flops | bytes accessed | tf_op | source)
XLA Modules:
  0.0 231.8 jit_solution(3247410838116859868)
XLA Ops:
  6.5 2.5 %fusion.10 = bf16[1,256,256]{2,1,0:T(8,128)(2,1)} fusion(bf16[12,256,128]{2,1,0:T(8,128)(2,1)} %param.17, bf16[12,128,256]{2,1,0:T(8,128)(2,1)} %param.13), kind=kOutput, calls=%fused_computation.20 | convolution fusion | flops 201392128 | bytes 1703936 | tf_op jit(solution)/shard_map/bcp,bpr->cr/dot_general | solution.py:80
  9.0 0.0 all-reduce.2.cloned.1.call-update
  9.1 0.0 all-gather.3.cloned.1.call-start
  9.1 0.7 all-gather.3.cloned.1.call-update
  9.8 0.0 all-gather.5.cloned.1.call-start
  9.8 46.2 %all-reduce.2.cloned.1.call-done = bf16[1,256,256]{2,1,0:T(8,128)(2,1)} async-done(((bf16[1,256,256]{2,1,0:T(8,128)(2,1)}), bf16[1,256,256]{2,1,0:T(8,128)(2,1)}) %all-reduce.2.cloned.1.call-update) | async-done | bytes 131088 | tf_op jit(solution)/shard_map/psum | solution.py:84
  56.0 0.0 all-gather.5.cloned.1.call-update
  56.0 46.2 %all-gather.3.cloned.1.call-done = bf16[48,128,256]{2,1,0:T(8,128)(2,1)} async-done(((bf16[12,128,256]{2,1,0:T(8,128)(2,1)}), bf16[48,128,256]{2,1,0:T(8,128)(2,1)}) %all-gather.3.cloned.1.call-update) | async-done | bytes 3145744 | tf_op jit(solution)/shard_map/all_gather | solution.py:72
  102.2 5.1 %collective-permute-start = (bf16[48,128,256]{2,1,0:T(8,128)(2,1)}, bf16[48,128,256]{2,1,0:T(8,128)(2,1)}, u32[]{:S(2)}, u32[]{:S(2)}) collective-permute-start(bf16[48,128,256]{2,1,0:T(8,128)(2,1)} %all-gather.3.cloned.1.call-done), channel_id=1, source_target_pairs={{0,4},{4,8},{8,12},{12,16},{16,20},{20,24},{24,28},{28,32},{32,36}... | collective-permute-start | bytes 9437192 | tf_op jit(solution)/shard_map/ppermute | solution.py:15
  107.3 1.9 collective-permute-start.1
  109.3 0.7 fusion.15
  110.0 0.0 copy-start.3
  110.0 0.0 copy-start.6
  110.0 0.0 copy-start.4
  110.0 2.9 %gather_fusion.1 = bf16[32,256,256]{2,1,0:T(8,128)(2,1)} fusion(bf16[8,256,256]{2,1,0:T(8,128)(2,1)S(1)} %copy-done, s32[1024]{0:T(1024)S(1)} %pad_clamp_fusion.3), kind=kCustom, calls=%fused_computation.1 | custom fusion | bytes 8388736 | tf_op jit(solution)/shard_map/gather | solution.py:48
  112.9 0.6 gather_fusion.3
  113.6 0.1 reshape.140
  113.7 0.1 fusion.14
  113.8 33.0 %collective-permute-done = bf16[48,128,256]{2,1,0:T(8,128)(2,1)} collective-permute-done((bf16[48,128,256]{2,1,0:T(8,128)(2,1)}, bf16[48,128,256]{2,1,0:T(8,128)(2,1)}, u32[]{:S(2)}, u32[]{:S(2)}) %collective-permute-start) | collective-permute-done | bytes 3145760 | tf_op jit(solution)/shard_map/ppermute | solution.py:15
  146.8 7.7 %collective-permute-done.1 = bf16[48,128,256]{2,1,0:T(8,128)(2,1)} collective-permute-done((bf16[48,128,256]{2,1,0:T(8,128)(2,1)}, bf16[48,128,256]{2,1,0:T(8,128)(2,1)}, u32[]{:S(2)}, u32[]{:S(2)}) %collective-permute-start.1) | collective-permute-done | bytes 3145760 | tf_op jit(solution)/shard_map/ppermute | solution.py:17
  154.5 8.4 %pad_maximum_fusion = bf16[144,128,256]{2,1,0:T(8,128)(2,1)} fusion(bf16[48,128,256]{2,1,0:T(8,128)(2,1)} %collective-permute-done.1, bf16[48,128,256]{2,1,0:T(8,128)(2,1)} %all-gather.3.cloned.1.call-done, bf16[48,128,256]{2,1,0:T(8,128)(2,1)} %collective-permute-done), kind=kLoop, calls=%fused_computation.7 | loop fusion | flops 9437184 | bytes 18874368 | tf_op jit(solution)/shard_map/concatenate | solution.py:13
  162.9 12.0 %gather_fusion = bf16[192,128,256]{2,1,0:T(8,128)(2,1)} fusion(bf16[144,128,256]{2,1,0:T(8,128)(2,1)} %pad_maximum_fusion, s32[1024]{0:T(1024)S(1)} %pad_clamp_fusion.4), kind=kCustom, calls=%fused_computation | custom fusion | bytes 25166592 | tf_op jit(solution)/shard_map/gather | solution.py:74
  174.9 16.8 %copy.16 = bf16[12,16,128,256]{2,3,1,0:T(8,128)(2,1)} copy(bf16[12,16,128,256]{3,2,1,0:T(8,128)(2,1)} %bitcast.66) | data formatting | bytes 25165824 | tf_op jit(solution)/shard_map/gather | solution.py:74
  191.6 6.1 %gather_fusion.2 = bf16[32,256,256]{2,1,0:T(8,128)(2,1)} fusion(bf16[64,256,256]{2,1,0:T(8,128)(2,1)} %all-gather.5.cloned.1.call-done, s32[1024]{0:T(1024)S(1)} %pad_clamp_fusion.2), kind=kCustom, calls=%fused_computation.2 | custom fusion | bytes 8388736 | tf_op jit(solution)/shard_map/gather | solution.py:49
  197.8 5.3 %convolution_bitcast_fusion.1 = f32[256,256]{0,1:T(8,128)S(1)} fusion(bf16[32,256,256]{2,1,0:T(8,128)(2,1)} %gather_fusion.1, bf16[32,256,256]{2,1,0:T(8,128)(2,1)} %gather_fusion.2), kind=kOutput, calls=%fused_computation.14 | convolution fusion | flops 1073741824 | bytes 8650752 | tf_op jit(solution)/shard_map/kcd,kdr->cr/dot_general | solution.py:46
  203.1 0.5 copy-done.2
  203.6 3.7 %fusion.5 = bf16[8,256,256]{1,2,0:T(8,128)(2,1)S(1)} fusion(bf16[8,8,256,256]{3,2,1,0:T(8,128)(2,1)S(1)} %bitcast.67, bf16[8,256,256]{2,1,0:T(8,128)(2,1)} %param.19), kind=kOutput, calls=%fused_computation.11 | convolution fusion | flops 2148007936 | bytes 10485760 | tf_op jit(solution)/shard_map/get,kgtv->kev/dot_general | solution.py:37
  207.3 0.6 gather_fusion.4
  207.9 1.7 fusion.9
  209.6 1.5 fusion.20
  211.2 11.1 %bitcast_add_fusion = f32[12,128,256]{1,2,0:T(8,128)} fusion(f32[256,12,128]{2,0,1:T(8,128)S(1)} %fusion.20, bf16[12,16,128,128]{3,2,1,0:T(8,128)(2,1)} %param.14, bf16[12,16,128,256]{2,3,1,0:T(8,128)(2,1)} %copy.16, bf16[12,16]{1,0:T(8,128)(2,1)S(1)} %fusion.14), kind=kOutput, calls=%fused_computation.10 | convolution fusion | flops 1617297408 | bytes 22020480 | tf_op jit(solution)/shard_map/bkpq,bkqr->bpr/dot_general | solution.py:79
  222.3 3.0 %copy.17 = f32[12,128,256]{2,1,0:T(8,128)} copy(f32[12,128,256]{1,2,0:T(8,128)} %bitcast_add_fusion) | data formatting | bytes 3145728 | tf_op jit(solution)/shard_map/add | solution.py:98
  (23 shorter events, 0.1 us)
Async XLA Ops:
  6.5 103.4 %copy-start = (bf16[8,256,256]{2,1,0:T(8,128)(2,1)S(1)}, bf16[8,256,256]{2,1,0:T(8,128)(2,1)}, u32[]{:S(2)}) copy-start(bf16[8,256,256]{2,1,0:T(8,128)(2,1)} %param.21) | copy-start | bytes 3145732
  6.5 49.5 %all-reduce.2.cloned.1.call-start = ((), (), s32[]{:S(2)}) async-start(), calls=%async_computation.1 | async-start | bytes 262144 | tf_op jit(solution)/shard_map/psum | solution.py:84
  9.1 93.2 %all-gather.3.cloned.1.call-start = ((), (), s32[]{:S(2)}) async-start(), calls=%async_computation | async-start | bytes 3932160 | tf_op jit(solution)/shard_map/all_gather | solution.py:72
  9.8 181.8 %all-gather.5.cloned.1.call-start = ((), (), s32[]{:S(2)}) async-start(), calls=%async_computation.2 | async-start | bytes 8519680 | tf_op jit(solution)/shard_map/all_gather | solution.py:85
  102.2 44.5 %collective-permute-start = (bf16[48,128,256]{2,1,0:T(8,128)(2,1)}, bf16[48,128,256]{2,1,0:T(8,128)(2,1)}, u32[]{:S(2)}, u32[]{:S(2)}) collective-permute-start(bf16[48,128,256]{2,1,0:T(8,128)(2,1)} %all-gather.3.cloned.1.call-done), channel_id=1, source_target_pairs={{0,4},{4,8},{8,12},{12,16},{16,20},{20,24},{24,28},{28,32},{32,36}... | collective-permute-start | bytes 9437192 | tf_op jit(solution)/shard_map/ppermute | solution.py:15
  107.3 47.1 %collective-permute-start.1 = (bf16[48,128,256]{2,1,0:T(8,128)(2,1)}, bf16[48,128,256]{2,1,0:T(8,128)(2,1)}, u32[]{:S(2)}, u32[]{:S(2)}) collective-permute-start(bf16[48,128,256]{2,1,0:T(8,128)(2,1)} %all-gather.3.cloned.1.call-done), channel_id=1, source_target_pairs={{4,0},{8,4},{12,8},{16,12},{20,16},{24,20},{28,24},{32,28},{36,32}... | collective-permute-start | bytes 9437192 | tf_op jit(solution)/shard_map/ppermute | solution.py:17
  110.0 2.9 %copy-start.5 = (s32[1,8]{1,0:T(1,128)S(1)}, s32[1,8]{1,0:T(1,128)}, u32[]{:S(2)}) copy-start(s32[1,8]{1,0:T(1,128)} %param.25) | copy-start | bytes 100
  110.0 3.6 %copy-start.3 = (s32[12,16]{1,0:T(8,128)S(1)}, s32[12,16]{1,0:T(8,128)}, u32[]{:S(2)}) copy-start(s32[12,16]{1,0:T(8,128)} %param.15) | copy-start | bytes 2308
  110.0 3.6 %copy-start.6 = (s32[1,32]{1,0:T(1,128)S(1)}, s32[1,32]{1,0:T(1,128)}, u32[]{:S(2)}) copy-start(s32[1,32]{1,0:T(1,128)} %param.22) | copy-start | bytes 388
  110.0 3.7 %copy-start.7 = (s32[1,8]{1,0:T(1,128)S(1)}, s32[1,8]{1,0:T(1,128)}, u32[]{:S(2)}) copy-start(s32[1,8]{1,0:T(1,128)} %param.24) | copy-start | bytes 100
  110.0 3.7 %copy-start.4 = (s32[12]{0:T(128)S(1)}, s32[12]{0:T(128)}, u32[]{:S(2)}) copy-start(s32[12]{0:T(128)} %param.16) | copy-start | bytes 148
  197.8 5.8 %copy-start.2 = (bf16[64,256,256]{2,1,0:T(8,128)(2,1)S(1)}, bf16[64,256,256]{2,1,0:T(8,128)(2,1)}, u32[]{:S(2)}) copy-start(bf16[64,256,256]{2,1,0:T(8,128)(2,1)} %all-gather.5.cloned.1.call-done) | copy-start | bytes 25165828
  211.1 14.2 %copy-start.1 = (bf16[8,256,256]{2,1,0:T(8,128)(2,1)S(1)}, bf16[8,256,256]{2,1,0:T(8,128)(2,1)}, u32[]{:S(2)}) copy-start(bf16[8,256,256]{2,1,0:T(8,128)(2,1)} %param.21) | copy-start | bytes 3145732
Sparse Core Ops, SparseCore 0:
  9.6 46.3 all-reduce.1
  57.8 44.3 all-gather.2
  105.0 81.0 all-gather.4
where the time goes:
time: 233 us; the launch traced here: 232 us
  waiting for transfers between devices  134 us (58%)
  local copies, waits for them, and re-layouts  42.6 us (18%)
  matrix products  25.9 us (11%)
  between operations  13.3 us (6%)
  other arithmetic  9.2 us (4%)
  starting transfers between devices  7.09 us (3%)
    all_gather x1, waiting for transfers between devices, on_device(): subtree = lax.all_gather(charges, 'level', axis=0, tiled=True)  46.2 us
    psum x1, waiting for transfers between devices, on_device(): moment = lax.psum(partial_moment.astype(jnp.bfloat16), 'level')  46.2 us
    ppermute x1, waiting for transfers between devices, extended_2(): lax.ppermute(tail, axis, [(i, (i + 1) % count) for i in range(ends)])  33 us
    gather x2, local copies, waits for them, and re-layouts, on_device(): picked = extended[near_source]  28.7 us
    dot_general x1, matrix products, on_device(): jnp.einsum('bkpq,bkqr->bpr', near_mat, picked, preferred_element_type=jnp...  11.1 us
    concatenate x1, other arithmetic, extended_2(): jnp.concatenate([lax.ppermute(tail, axis, [(i, (i + 1) % count) for i in...  8.42 us
    ppermute x1, waiting for transfers between devices, extended_2(): lax.ppermute(head, axis, [((i + 1) % count, i) for i in range(ends)])  7.72 us
    gather x1, local copies, waits for them, and re-layouts, top_tree(): every[subtree_interaction_list[0]]  6.13 us
  transfers between devices with their start and end apart: 5, of which 4 were waited for; matrix products, arithmetic and copies ran while one was open for 18% of the time, Pallas kernels for 0%

commit v1 on v0

--- a/solution.py
+++ b/solution.py
@@ -2,6 +2,12 @@
 import jax.numpy as jnp
 from jax import lax
 from jax.sharding import PartitionSpec as P
+
+
+def add_all(shard, mesh_axis):
+    shards = lax.all_gather(shard, mesh_axis, axis=0, tiled=False)
+    summed = shards.sum(axis=0)
+    return summed
 
 
 def extended_2(cells, sides, width):
@@ -81,7 +87,7 @@
         "bcp,bpr->cr", moment_map, charges, preferred_element_type=jnp.float32
     )
     leaf_index = lax.axis_index("leaf")
-    moment = lax.psum(partial_moment.astype(jnp.bfloat16), "level")
+    moment = add_all(partial_moment.astype(jnp.bfloat16), "level")
     every = lax.all_gather(moment[None], "leaf", axis=0, tiled=True)
     local_part = top_tree(
         every,

time: 233 us -> 184 us (0.79)
  waiting for transfers between devices: 134 us -> 72.7 us
  blocking collectives: 0 us -> 11.8 us
    psum x1 -> x0, waiting for transfers between devices: 46.2 us -> none  [on_device(): moment = lax.psum(partial_moment.astype(jnp.bfloat16), 'level')]
    all_gather x1, waiting for transfers between devices: 46.2 us -> 31.3 us  [on_device(): subtree = lax.all_gather(charges, 'level', axis=0, tiled=True)]
    all_gather x0 -> x1, blocking collectives: none -> 11.8 us  [add_all(): shards = lax.all_gather(shard, mesh_axis, axis=0, tiled=False)]
  transfers between devices with their start and end apart: 5 -> 4, of which waited for: 4 -> 3; matrix products, arithmetic and copies ran while one was open for 18% -> 24% of each run, Pallas kernels for 0% -> 0%
where the time goes in v1:
time: 184 us; the launch traced here: 183 us
  waiting for transfers between devices  72.7 us (40%)
  local copies, waits for them, and re-layouts  42.5 us (23%)
  matrix products  25.1 us (14%)
  between operations  13.6 us (7%)
  blocking collectives  11.8 us (6%)
  other arithmetic  9.94 us (5%)
  starting transfers between devices  7.05 us (4%)
    ppermute x1, waiting for transfers between devices, extended_2(): lax.ppermute(tail, axis, [(i, (i + 1) % count) for i in range(ends)])  33 us
    all_gather x1, waiting for transfers between devices, on_device(): subtree = lax.all_gather(charges, 'level', axis=0, tiled=True)  31.3 us
    gather x2, local copies, waits for them, and re-layouts, on_device(): picked = extended[near_source]  28.7 us
    all_gather x1, blocking collectives, add_all(): shards = lax.all_gather(shard, mesh_axis, axis=0, tiled=False)  11.8 us
    dot_general x1, matrix products, on_device(): jnp.einsum('bkpq,bkqr->bpr', near_mat, picked, preferred_element_type=jnp...  11.1 us
    concatenate x1, other arithmetic, extended_2(): jnp.concatenate([lax.ppermute(tail, axis, [(i, (i + 1) % count) for i in...  8.41 us
    ppermute x1, waiting for transfers between devices, extended_2(): lax.ppermute(head, axis, [((i + 1) % count, i) for i in range(ends)])  7.72 us
    gather x1, local copies, waits for them, and re-layouts, top_tree(): every[subtree_interaction_list[0]]  6.12 us
  transfers between devices with their start and end apart: 4, of which 3 were waited for; matrix products, arithmetic and copies ran while one was open for 24% of the time, Pallas kernels for 0%

profile of v1, /device:TPU:103, one launch (start us, length us, event | category | flops | bytes accessed | tf_op | source)
XLA Modules:
  0.0 182.7 jit_solution(17348469819178732740)
XLA Ops:
  6.5 0.7 all-gather.5.cloned.1.call-update
  7.3 0.0 all-gather.7.cloned.1.call-start
  7.3 1.7 fusion.7
  9.0 11.8 %all-gather = bf16[1024,256]{1,0:T(8,128)(2,1)S(1)} all-gather(bf16[256,256]{1,0:T(8,128)(2,1)S(1)} %fusion.7), channel_id=2, replica_groups=mesh['leaf'=64,'level'=4] {'level'}, dimensions={0}, use_global_device_ids=true | all-gather | bytes 655360 | tf_op jit(solution)/shard_map/all_gather | solution.py:8
  20.8 0.7 reduce_sum.12
  21.6 0.0 all-gather.7.cloned.1.call-update
  21.6 31.3 %all-gather.5.cloned.1.call-done = bf16[48,128,256]{2,1,0:T(8,128)(2,1)} async-done(((bf16[12,128,256]{2,1,0:T(8,128)(2,1)}), bf16[48,128,256]{2,1,0:T(8,128)(2,1)}) %all-gather.5.cloned.1.call-update) | async-done | bytes 3145744 | tf_op jit(solution)/shard_map/all_gather | solution.py:78
  52.9 5.1 %collective-permute-start = (bf16[48,128,256]{2,1,0:T(8,128)(2,1)}, bf16[48,128,256]{2,1,0:T(8,128)(2,1)}, u32[]{:S(2)}, u32[]{:S(2)}) collective-permute-start(bf16[48,128,256]{2,1,0:T(8,128)(2,1)} %all-gather.5.cloned.1.call-done), channel_id=1, source_target_pairs={{0,4},{4,8},{8,12},{12,16},{16,20},{20,24},{24,28},{28,32},{32,36}... | collective-permute-start | bytes 9437192 | tf_op jit(solution)/shard_map/ppermute | solution.py:21
  58.0 1.9 %collective-permute-start.1 = (bf16[48,128,256]{2,1,0:T(8,128)(2,1)}, bf16[48,128,256]{2,1,0:T(8,128)(2,1)}, u32[]{:S(2)}, u32[]{:S(2)}) collective-permute-start(bf16[48,128,256]{2,1,0:T(8,128)(2,1)} %all-gather.5.cloned.1.call-done), channel_id=1, source_target_pairs={{4,0},{8,4},{12,8},{16,12},{20,16},{24,20},{28,24},{32,28},{36,32}... | collective-permute-start | bytes 9437192 | tf_op jit(solution)/shard_map/ppermute | solution.py:23
  59.9 0.7 fusion.14
  60.6 0.0 copy-start.5
  60.6 0.0 copy-start.3
  60.6 0.0 copy-start.4
  60.7 2.9 %gather_fusion.1 = bf16[32,256,256]{2,1,0:T(8,128)(2,1)} fusion(bf16[8,256,256]{2,1,0:T(8,128)(2,1)S(1)} %copy-done, s32[1024]{0:T(1024)S(1)} %pad_clamp_fusion.3), kind=kCustom, calls=%fused_computation.1 | custom fusion | bytes 8388736 | tf_op jit(solution)/shard_map/gather | solution.py:54
  63.6 0.6 gather_fusion.3
  64.2 0.1 reshape.140
  64.4 0.1 fusion.13
  64.4 33.0 %collective-permute-done = bf16[48,128,256]{2,1,0:T(8,128)(2,1)} collective-permute-done((bf16[48,128,256]{2,1,0:T(8,128)(2,1)}, bf16[48,128,256]{2,1,0:T(8,128)(2,1)}, u32[]{:S(2)}, u32[]{:S(2)}) %collective-permute-start) | collective-permute-done | bytes 3145760 | tf_op jit(solution)/shard_map/ppermute | solution.py:21
  97.4 7.7 %collective-permute-done.1 = bf16[48,128,256]{2,1,0:T(8,128)(2,1)} collective-permute-done((bf16[48,128,256]{2,1,0:T(8,128)(2,1)}, bf16[48,128,256]{2,1,0:T(8,128)(2,1)}, u32[]{:S(2)}, u32[]{:S(2)}) %collective-permute-start.1) | collective-permute-done | bytes 3145760 | tf_op jit(solution)/shard_map/ppermute | solution.py:23
  105.1 8.4 %pad_maximum_fusion = bf16[144,128,256]{2,1,0:T(8,128)(2,1)} fusion(bf16[48,128,256]{2,1,0:T(8,128)(2,1)} %collective-permute-done.1, bf16[48,128,256]{2,1,0:T(8,128)(2,1)} %all-gather.5.cloned.1.call-done, bf16[48,128,256]{2,1,0:T(8,128)(2,1)} %collective-permute-done), kind=kLoop, calls=%fused_computation.7 | loop fusion | flops 9437184 | bytes 18874368 | tf_op jit(solution)/shard_map/concatenate | solution.py:19
  113.5 11.9 %gather_fusion = bf16[192,128,256]{2,1,0:T(8,128)(2,1)} fusion(bf16[144,128,256]{2,1,0:T(8,128)(2,1)} %pad_maximum_fusion, s32[1024]{0:T(1024)S(1)} %pad_clamp_fusion.4), kind=kCustom, calls=%fused_computation | custom fusion | bytes 25166592 | tf_op jit(solution)/shard_map/gather | solution.py:80
  125.5 16.7 %copy.16 = bf16[12,16,128,256]{2,3,1,0:T(8,128)(2,1)} copy(bf16[12,16,128,256]{3,2,1,0:T(8,128)(2,1)} %bitcast.64) | data formatting | bytes 25165824 | tf_op jit(solution)/shard_map/gather | solution.py:80
  142.2 6.1 %gather_fusion.2 = bf16[32,256,256]{2,1,0:T(8,128)(2,1)} fusion(bf16[64,256,256]{2,1,0:T(8,128)(2,1)} %bitcast.66, s32[1024]{0:T(1024)S(1)} %pad_clamp_fusion.2), kind=kCustom, calls=%fused_computation.2 | custom fusion | bytes 8388736 | tf_op jit(solution)/shard_map/gather | solution.py:55
  148.3 5.3 %convolution_bitcast_fusion.1 = f32[256,256]{0,1:T(8,128)S(1)} fusion(bf16[32,256,256]{2,1,0:T(8,128)(2,1)} %gather_fusion.1, bf16[32,256,256]{2,1,0:T(8,128)(2,1)} %gather_fusion.2), kind=kOutput, calls=%fused_computation.14 | convolution fusion | flops 1073741824 | bytes 8650752 | tf_op jit(solution)/shard_map/kcd,kdr->cr/dot_general | solution.py:52
  153.7 0.5 copy-done.2
  154.2 3.7 %fusion.5 = bf16[8,256,256]{1,2,0:T(8,128)(2,1)S(1)} fusion(bf16[8,8,256,256]{3,2,1,0:T(8,128)(2,1)S(1)} %bitcast.67, bf16[8,256,256]{2,1,0:T(8,128)(2,1)} %param.19), kind=kOutput, calls=%fused_computation.11 | convolution fusion | flops 2148007936 | bytes 10485760 | tf_op jit(solution)/shard_map/get,kgtv->kev/dot_general | solution.py:43
  157.9 0.6 gather_fusion.4
  158.5 1.7 fusion.9
  160.2 1.5 fusion.19
  161.7 0.0 copy-start.1
  161.7 11.1 %bitcast_add_fusion = f32[12,128,256]{1,2,0:T(8,128)} fusion(f32[256,12,128]{2,0,1:T(8,128)S(1)} %fusion.19, bf16[12,16,128,128]{3,2,1,0:T(8,128)(2,1)} %param.14, bf16[12,16,128,256]{2,3,1,0:T(8,128)(2,1)} %copy.16, bf16[12,16]{1,0:T(8,128)(2,1)S(1)} %fusion.13), kind=kOutput, calls=%fused_computation.10 | convolution fusion | flops 1617297408 | bytes 22020480 | tf_op jit(solution)/shard_map/bkpq,bkqr->bpr/dot_general | solution.py:85
  172.9 3.0 %copy.17 = f32[12,128,256]{2,1,0:T(8,128)} copy(f32[12,128,256]{1,2,0:T(8,128)} %bitcast_add_fusion) | data formatting | bytes 3145728 | tf_op jit(solution)/shard_map/add | solution.py:104
  (22 shorter events, 0.1 us)
Async XLA Ops:
  6.5 54.1 %copy-start = (bf16[8,256,256]{2,1,0:T(8,128)(2,1)S(1)}, bf16[8,256,256]{2,1,0:T(8,128)(2,1)}, u32[]{:S(2)}) copy-start(bf16[8,256,256]{2,1,0:T(8,128)(2,1)} %param.21) | copy-start | bytes 3145732
  6.5 46.3 %all-gather.5.cloned.1.call-start = ((), (), s32[]{:S(2)}) async-start(), calls=%async_computation | async-start | bytes 3932160 | tf_op jit(solution)/shard_map/all_gather | solution.py:78
  7.3 135.0 %all-gather.7.cloned.1.call-start = ((), (), s32[]{:S(2)}) async-start(), calls=%async_computation.1 | async-start | bytes 8519680 | tf_op jit(solution)/shard_map/all_gather | solution.py:91
  52.9 44.5 %collective-permute-start = (bf16[48,128,256]{2,1,0:T(8,128)(2,1)}, bf16[48,128,256]{2,1,0:T(8,128)(2,1)}, u32[]{:S(2)}, u32[]{:S(2)}) collective-permute-start(bf16[48,128,256]{2,1,0:T(8,128)(2,1)} %all-gather.5.cloned.1.call-done), channel_id=1, source_target_pairs={{0,4},{4,8},{8,12},{12,16},{16,20},{20,24},{24,28},{28,32},{32,36}... | collective-permute-start | bytes 9437192 | tf_op jit(solution)/shard_map/ppermute | solution.py:21
  58.0 47.1 %collective-permute-start.1 = (bf16[48,128,256]{2,1,0:T(8,128)(2,1)}, bf16[48,128,256]{2,1,0:T(8,128)(2,1)}, u32[]{:S(2)}, u32[]{:S(2)}) collective-permute-start(bf16[48,128,256]{2,1,0:T(8,128)(2,1)} %all-gather.5.cloned.1.call-done), channel_id=1, source_target_pairs={{4,0},{8,4},{12,8},{16,12},{20,16},{24,20},{28,24},{32,28},{36,32}... | collective-permute-start | bytes 9437192 | tf_op jit(solution)/shard_map/ppermute | solution.py:23
  60.6 2.9 %copy-start.5 = (s32[1,8]{1,0:T(1,128)S(1)}, s32[1,8]{1,0:T(1,128)}, u32[]{:S(2)}) copy-start(s32[1,8]{1,0:T(1,128)} %param.25) | copy-start | bytes 100
  60.6 3.6 %copy-start.3 = (s32[12,16]{1,0:T(8,128)S(1)}, s32[12,16]{1,0:T(8,128)}, u32[]{:S(2)}) copy-start(s32[12,16]{1,0:T(8,128)} %param.15) | copy-start | bytes 2308
  60.6 3.7 %copy-start.6 = (s32[1,32]{1,0:T(1,128)S(1)}, s32[1,32]{1,0:T(1,128)}, u32[]{:S(2)}) copy-start(s32[1,32]{1,0:T(1,128)} %param.22) | copy-start | bytes 388
  60.6 3.7 %copy-start.7 = (s32[1,8]{1,0:T(1,128)S(1)}, s32[1,8]{1,0:T(1,128)}, u32[]{:S(2)}) copy-start(s32[1,8]{1,0:T(1,128)} %param.24) | copy-start | bytes 100
  60.6 3.7 %copy-start.4 = (s32[12]{0:T(128)S(1)}, s32[12]{0:T(128)}, u32[]{:S(2)}) copy-start(s32[12]{0:T(128)} %param.16) | copy-start | bytes 148
  148.3 5.8 %copy-start.2 = (bf16[16384,256]{1,0:T(8,128)(2,1)S(1)}, bf16[16384,256]{1,0:T(8,128)(2,1)}, u32[]{:S(2)}) copy-start(bf16[16384,256]{1,0:T(8,128)(2,1)} %all-gather.7.cloned.1.call-done) | copy-start | bytes 25165828
  161.7 14.1 %copy-start.1 = (bf16[8,256,256]{2,1,0:T(8,128)(2,1)S(1)}, bf16[8,256,256]{2,1,0:T(8,128)(2,1)}, u32[]{:S(2)}) copy-start(bf16[8,256,256]{2,1,0:T(8,128)(2,1)} %param.21) | copy-start | bytes 3145732
Sparse Core Ops, SparseCore 0:
  9.1 43.6 all-gather.4
  55.6 81.0 all-gather.6
